TPU v7x, 512 devices: a whole 4x4x16 slice. The times are simulated.
512 devices in a mesh: dp: 16 (over z), expert: 32 (over y, x, core).
Axes of the slice: x: 4, y: 4, z: 16, core: 2. Of those that a mesh axis runs over, the one named last changes fastest.
Arguments:
- tokens: bfloat16 [2048, 4096], P('dp', 'expert'), may hold values from -6 to 6
- norm_gain: float32 [4096], replicated, may hold values from 0.1 to 1.9
- routes: int32 [2048, 2], P('dp'), may hold values from 0 to 31, all different within a row; in each aligned block of 128 rows (0 to 127, 128 to 255, ...) at most 10 rows name the same one
- route_prob: float32 [2048, 2], P('dp'), may hold values from 0.2 to 1
- gate_weight: bfloat16 [32, 4096, 2048], P('expert', None, 'dp'), may hold values from -0.09375 to 0.09375
- up_weight: bfloat16 [32, 4096, 2048], P('expert', None, 'dp'), may hold values from -0.09375 to 0.09375
- down_weight: bfloat16 [32, 2048, 4096], P('expert', 'dp'), may hold values from -0.125 to 0.125
- key_value_weight: bfloat16 [4096, 2048], P('expert'), may hold values from -0.09375 to 0.09375
- key_value_target: bfloat16 [2048, 2048], P('dp', 'expert'), may hold values from -6 to 6
- concept_mask: int32 [2048], P('dp'), may hold values 0 or 1
Outputs:
- down_grad: bfloat16 [32, 2048, 4096], P('expert', 'dp')
- key_value_grad: float32 [4096, 2048], P('expert', 'dp')
Inputs may be any that keep to these rules, and one draw needn't show every extreme that they name: `routes`: in each aligned block of 128 rows no expert is named by more than 10 rows; the two choices of a token differ.
All inputs are finite; a program needn't handle non-finite values. No bound on the sum of `concept_mask` on one device may be relied on, other than what follows from the above.
Results may differ from a plain program's by a relative error of at most 0.033.
Values may be sent and summed in bfloat16 or wider, within the bound.
No kernel may reach another device: no remote copies, remote signals or barrier semaphores. Data moves between devices by JAX's collectives and lax.ppermute only.
A program may use at most 64 MiB of HBM per device.

v0:
```python
import jax
import jax.numpy as jnp
from jax import lax
from jax.sharding import PartitionSpec as P

eps_norm = 1e-06


def slot_targets(routes, expert_count, capacity):
    flat = routes.reshape(-1)
    onehot = (flat[:, None] == jnp.arange(expert_count, dtype=jnp.int32)[None, :]).astype(jnp.int32)
    before = jnp.cumsum(onehot, axis=0) - onehot
    return flat * capacity + jnp.sum(before * onehot, axis=1)


def per_device(
    tokens,
    norm_gain,
    routes,
    route_prob,
    gate_weight,
    up_weight,
    down_weight,
    key_value_weight,
    key_value_target,
    concept_mask,
):
    token_rows, width = tokens.shape
    top_count = routes.shape[1]
    expert_count = lax.axis_size("expert")
    capacity = 5 * token_rows * top_count // (4 * expert_count)
    model_width = width * expert_count
    position = slot_targets(routes, expert_count, capacity)
    prob_flat = route_prob.reshape(-1)

    def place_rows(pair_rows):
        filled = (
            jnp.zeros((expert_count * capacity, width), jnp.bfloat16).at[position].set(pair_rows)
        )
        return filled.reshape(expert_count, capacity, width)

    values = tokens.astype(jnp.float32)
    total_sq = lax.psum(jnp.sum(values * values, axis=1), "expert")
    scale = lax.rsqrt(total_sq / model_width + eps_norm)
    local_gain = lax.dynamic_slice_in_dim(norm_gain, lax.axis_index("expert") * width, width)
    outgoing = (values * scale[:, None] * local_gain[None, :]).astype(jnp.bfloat16)
    send_slots = place_rows(jnp.repeat(outgoing, top_count, axis=0))
    arrived = lax.all_to_all(send_slots, "expert", split_axis=0, concat_axis=2, tiled=True)[0]
    rows = lax.all_gather(arrived, "dp", axis=0, tiled=True)
    gate_val = jnp.dot(rows, gate_weight[0], preferred_element_type=jnp.float32)
    up_val = jnp.dot(rows, up_weight[0], preferred_element_type=jnp.float32)
    hidden = (jax.nn.silu(gate_val) * up_val).astype(jnp.bfloat16)
    expert_out = lax.psum_scatter(
        jnp.dot(hidden, down_weight[0], preferred_element_type=jnp.float32).astype(jnp.bfloat16),
        "dp",
        scatter_dimension=0,
        tiled=True,
    )
    returned = lax.all_to_all(expert_out[None], "expert", split_axis=2, concat_axis=0, tiled=True)
    picked = returned.reshape(expert_count * capacity, width)[position].astype(jnp.float32)
    expert_mix = (picked * prob_flat[:, None]).reshape(token_rows, top_count, width).sum(axis=1)
    state = (tokens.astype(jnp.float32) + expert_mix).astype(jnp.bfloat16)
    proj_term = jnp.dot(state, key_value_weight, preferred_element_type=jnp.float32)
    proj_cols = lax.psum_scatter(
        proj_term.astype(jnp.bfloat16), "expert", scatter_dimension=1, tiled=True
    ).astype(jnp.float32)
    mask_col = concept_mask.astype(jnp.float32)[:, None]
    cotangent_cols = (
        mask_col * (proj_cols - key_value_target.astype(jnp.float32)) * token_rows ** (-0.5)
    ).astype(jnp.bfloat16)
    cotangent = lax.all_gather(cotangent_cols, "expert", axis=1, tiled=True)
    grad_term = jnp.einsum("tw,tk->wk", state, cotangent, preferred_element_type=jnp.float32)
    key_value_grad = lax.psum_scatter(
        grad_term.astype(jnp.bfloat16), "dp", scatter_dimension=1, tiled=True
    ).astype(jnp.float32)
    state_grad = jnp.einsum(
        "tk,wk->tw", cotangent, key_value_weight, preferred_element_type=jnp.float32
    )
    pair_grad = (jnp.repeat(state_grad, top_count, axis=0) * prob_flat[:, None]).astype(
        jnp.bfloat16
    )
    grad_slots = place_rows(pair_grad)
    landed = lax.all_to_all(grad_slots, "expert", split_axis=0, concat_axis=2, tiled=True)[0]
    down_total = jnp.einsum(
        "rf,rd->fd",
        hidden,
        lax.all_gather(landed, "dp", axis=0, tiled=True),
        preferred_element_type=jnp.float32,
    )
    return (down_total.astype(jnp.bfloat16)[None], key_value_grad)


def solution(mesh):
    placed = (
        P("dp", "expert"),
        P(),
        P("dp", None),
        P("dp", None),
        P("expert", None, "dp"),
        P("expert", None, "dp"),
        P("expert", "dp", None),
        P("expert", None),
        P("dp", "expert"),
        P("dp"),
    )
    return jax.shard_map(
        per_device,
        mesh=mesh,
        in_specs=placed,
        out_specs=(P("expert", "dp", None), P("expert", "dp")),
        check_vma=False,
    )
```

profile of v0, /device:TPU:2, one launch (start us, length us, event | category | flops | bytes accessed | tf_op | source)
XLA Modules:
  0.0 632.4 jit_solution(2933031377896465025)
XLA Ops:
  7.2 0.8 broadcast_multiply_fusion
  8.0 0.8 copy.34
  8.9 0.1 eq.25
  9.1 0.9 fusion.7
  9.9 63.0 %psum.7 = f32[128]{0:T(128)S(1)} all-reduce(f32[128]{0:T(128)S(1)} %fusion.7), channel_id=1, replica_groups=mesh['dp'=16,'expert'=32] {'expert'}, use_global_device_ids=true, to_apply=%region_4.5 | all-reduce | flops 128 | bytes 1024 | tf_op jit(solution)/shard_map/psum | solution.py:43
  73.0 0.1 mul.83
  73.2 0.6 reduce-window.6
  73.8 0.2 slice_reduce_fusion
  74.0 0.8 dynamic_slice.3
  74.8 0.8 fusion.9
  75.8 1.2 scatter_custom_fusion
  77.0 14.9 %all_to_all.45 = bf16[32,10,128]{2,1,0:T(8,128)(2,1)S(1)} all-to-all(bf16[32,10,128]{2,1,0:T(8,128)(2,1)S(1)} %reshape.83), channel_id=1, replica_groups=mesh['dp'=16,'expert'=32] {'expert'}, dimensions={0} | all-to-all | bytes 163840 | tf_op jit(solution)/shard_map/all_to_all | solution.py:48
  92.0 0.7 reshape.112
  92.8 74.1 %all-gather.5.cloned.1.call-done = bf16[16,10,4096]{2,1,0:T(8,128)(2,1)} async-done(((bf16[1,10,4096]{2,1,0:T(8,128)(2,1)}), bf16[16,10,4096]{2,1,0:T(8,128)(2,1)}) %all-gather.5.cloned.1.call-update) | async-done | bytes 1310736 | tf_op jit(solution)/shard_map/all_gather | solution.py:49
  166.9 1.8 reshape.113
  168.7 0.5 fusion.4
  169.2 0.7 copy-done.3
  170.0 0.5 fusion.1
  170.5 1.6 convolution_convert_fusion
  172.2 1.3 dynamic-slice
  174.1 135.3 %all-reduce.3.cloned.1.call-done = bf16[160,4096]{1,0:T(8,128)(2,1)} async-done(((bf16[160,4096]{1,0:T(8,128)(2,1)}), bf16[160,4096]{1,0:T(8,128)(2,1)}) %all-reduce.3.cloned.1.call-update) | async-done | bytes 1310736
  309.4 1.0 dynamic-slice_bitcast_fusion
  310.4 2.8 copy.38
  313.2 0.5 broadcast.74
  313.7 23.4 %reduce.2 = bf16[4096,10]{1,0:T(8,128)(2,1)} reduce(bf16[4096,1,10]{2,1,0:T(2,128)(2,1)S(1)} %bitcast.74, bf16[]{:T(256)} %broadcast.74), dimensions={1}, to_apply=%bitcast.60.reduce_sub_computation | reduce | bytes 163842
  337.1 3.4 reshape.126
  340.5 7.4 %all-to-all-start.1 = ((bf16[32,2,640]{2,1,0:T(2,128)(2,1)}), bf16[32,2,640]{2,1,0:T(2,128)(2,1)S(1)}, u32[]{:S(2)}, u32[]{:S(2)}) async-start(bf16[32,2,640]{2,1,0:T(2,128)(2,1)} %reshape.126), calls=%async_computation.1 | async-start | bytes 163840 | tf_op jit(solution)/shard_map/all_to_all | solution.py:59
  348.0 6.3 all-to-all-done.1
  354.3 2.2 reshape.127
  356.6 2.1 copy.39
  358.9 0.9 gather_fusion
  359.7 0.2 fusion.6
  360.0 1.1 convolution_convert_fusion.3
  361.2 93.7 %reduce-scatter.5.cloned.1.call-done = bf16[128,64]{0,1:T(8,128)(2,1)} async-done(((bf16[128,2048]{0,1:T(8,128)(2,1)}), bf16[128,64]{0,1:T(8,128)(2,1)}) %reduce-scatter.5.cloned.1.call-update) | async-done | bytes 16400 | tf_op jit(solution)/shard_map/reduce_scatter | solution.py:64
  455.0 0.7 multiply_convert_fusion.2
  455.7 23.2 %all_gather.10 = bf16[128,2048]{0,1:T(8,128)(2,1)S(1)} all-gather(bf16[128,64]{0,1:T(8,128)(2,1)S(1)} %multiply_convert_fusion.2), channel_id=1, replica_groups=mesh['dp'=16,'expert'=32] {'expert'}, dimensions={1}, use_global_device_ids=true | all-gather | bytes 540672 | tf_op jit(solution)/shard_map/all_gather | solution.py:71
  478.9 0.3 convolution_convert_fusion.2
  479.2 1.0 copy.44
  480.4 0.3 fusion.22
  480.8 1.3 scatter_custom_fusion.1
  482.1 12.6 %all_to_all.46 = bf16[32,10,128]{2,1,0:T(8,128)(2,1)S(1)} all-to-all(bf16[32,10,128]{2,1,0:T(8,128)(2,1)S(1)} %reshape.86), channel_id=1, replica_groups=mesh['dp'=16,'expert'=32] {'expert'}, dimensions={0} | all-to-all | bytes 163840 | tf_op jit(solution)/shard_map/all_to_all | solution.py:83
  494.7 0.7 reshape.114
  495.4 54.2 %reduce-scatter.7.cloned.1.call-done = bf16[128,128]{1,0:T(8,128)(2,1)} async-done(((bf16[2048,128]{1,0:T(8,128)(2,1)}), bf16[128,128]{1,0:T(8,128)(2,1)}) %reduce-scatter.7.cloned.1.call-update) | async-done | bytes 32784
  549.6 0.9 copy.45
  550.5 0.6 convert_element_type.74
  551.1 71.5 %all-gather.7.cloned.1.call-done = bf16[16,10,4096]{2,1,0:T(8,128)(2,1)} async-done(((bf16[1,10,4096]{2,1,0:T(8,128)(2,1)}), bf16[16,10,4096]{2,1,0:T(8,128)(2,1)}) %all-gather.7.cloned.1.call-update) | async-done | bytes 1310736 | tf_op jit(solution)/shard_map/all_gather | solution.py:87
  622.7 1.8 reshape.115
  624.5 1.4 fusion
  (47 shorter events, 1.3 us)
Async XLA Ops:
  7.2 163.3 %copy-start = (bf16[1,128,4096]{2,1,0:T(8,128)(2,1)S(1)}, bf16[1,128,4096]{2,1,0:T(8,128)(2,1)}, u32[]{:S(2)}) copy-start(bf16[1,128,4096]{2,1,0:T(8,128)(2,1)} %param.16) | copy-start | bytes 3145732
  7.2 159.7 %all-gather.5.cloned.1.call-start = ((), (), s32[]{:S(2)}) async-start(), calls=%async_computation.6 | async-start | bytes 2228224 | tf_op jit(solution)/shard_map/all_gather | solution.py:49
  92.7 76.0 %copy-start.2 = (bf16[1,4096,128]{2,1,0:T(8,128)(2,1)S(1)}, bf16[1,4096,128]{2,1,0:T(8,128)(2,1)}, u32[]{:S(2)}) copy-start(bf16[1,4096,128]{2,1,0:T(8,128)(2,1)} %param.14) | copy-start | bytes 3145732
  92.7 216.7 %all-reduce.3.cloned.1.call-start = ((), (), s32[]{:S(2)}) async-start(), calls=%async_computation.9 | async-start | bytes 2621440
  168.7 1.2 copy-start.3
  170.5 1.6 copy-start.6
  340.5 13.8 %all-to-all-start.1 = ((bf16[32,2,640]{2,1,0:T(2,128)(2,1)}), bf16[32,2,640]{2,1,0:T(2,128)(2,1)S(1)}, u32[]{:S(2)}, u32[]{:S(2)}) async-start(bf16[32,2,640]{2,1,0:T(2,128)(2,1)} %reshape.126), calls=%async_computation.1 | async-start | bytes 163840 | tf_op jit(solution)/shard_map/all_to_all | solution.py:59
  348.0 107.0 %reduce-scatter.5.cloned.1.call-start = ((), (), s32[]{:S(2)}) async-start(), calls=%async_computation.5 | async-start | bytes 540672 | tf_op jit(solution)/shard_map/reduce_scatter | solution.py:64
  358.7 1.3 copy-start.1
  358.7 1.3 copy-start.4
  358.8 2.4 copy-start.7
  358.8 96.2 %copy-start.5 = (bf16[128,64]{0,1:T(8,128)(2,1)S(1)}, bf16[128,64]{0,1:T(8,128)(2,1)}, u32[]{:S(2)}) copy-start(bf16[128,64]{0,1:T(8,128)(2,1)} %param.18) | copy-start | bytes 49156
  361.2 188.5 %reduce-scatter.7.cloned.1.call-start = ((), (), s32[]{:S(2)}) async-start(), calls=%async_computation.8 | async-start | bytes 557056
  480.2 142.4 %all-gather.7.cloned.1.call-start = ((), (), s32[]{:S(2)}) async-start(), calls=%async_computation.7 | async-start | bytes 2228224 | tf_op jit(solution)/shard_map/all_gather | solution.py:87
Sparse Core Ops, SparseCore 0:
  92.8 74.0 all-gather.4
  172.2 137.1 all-reduce.2
  361.3 93.6 reduce-scatter.4
  480.3 69.2 reduce-scatter.6
  551.8 70.8 all-gather.6
where the time goes:
time: 633 us; the launch traced here: 632 us
  waiting for transfers between devices  435 us (69%)
  blocking collectives  114 us (18%)
  other arithmetic  29.5 us (5%)
  local copies, waits for them, and re-layouts  25.8 us (4%)
  between operations  14.8 us (2%)
  starting transfers between devices  7.63 us (1%)
    unnamed x7, waiting for transfers between devices  190 us
    reduce_scatter x1, waiting for transfers between devices, per_device(): lax.psum_scatter(proj_term.astype(jnp.bfloat16), 'expert', scatter_dimens...  93.7 us
    all_gather x1, waiting for transfers between devices, per_device(): rows = lax.all_gather(arrived, 'dp', axis=0, tiled=True)  74.1 us
    all_gather x1, waiting for transfers between devices, per_device(): lax.all_gather(landed, 'dp', axis=0, tiled=True)  71.5 us
    psum x1, blocking collectives, per_device(): total_sq = lax.psum(jnp.sum(values * values, axis=1), 'expert')  63 us
    unnamed x1, other arithmetic  23.4 us
    all_gather x1, blocking collectives, per_device(): cotangent = lax.all_gather(cotangent_cols, 'expert', axis=1, tiled=True)  23.2 us
    unnamed x29, local copies, waits for them, and re-layouts  16 us
  transfers between devices with their start and end apart: 6, of which 6 were waited for; matrix products, arithmetic and copies ran while one was open for 1% of the time, Pallas kernels for 0%

commit v1 on v0

--- a/solution.py
+++ b/solution.py
@@ -4,6 +4,22 @@
 from jax.sharding import PartitionSpec as P
 
 eps_norm = 1e-06
+
+
+def product_in_turn(value, axis, dim, contribution):
+    length, index, span = (lax.axis_size(axis), lax.axis_index(axis), value.shape[dim])
+    right = [(i, (i + 1) % length) for i in range(length)]
+    left = [(i, (i - 1) % length) for i in range(length)]
+    half = length // 2
+    from_left = from_right = value
+    total = contribution(value, index * span)
+    for step in range(1, half + 1):
+        from_left = lax.ppermute(from_left, axis, right)
+        if step < length - half:
+            from_right = lax.ppermute(from_right, axis, left)
+            total = total + contribution(from_right, (index + step) % length * span)
+        total = total + contribution(from_left, (index - step) % length * span)
+    return total
 
 
 def slot_targets(routes, expert_count, capacity):
@@ -81,11 +97,16 @@
     )
     grad_slots = place_rows(pair_grad)
     landed = lax.all_to_all(grad_slots, "expert", split_axis=0, concat_axis=2, tiled=True)[0]
-    down_total = jnp.einsum(
-        "rf,rd->fd",
-        hidden,
-        lax.all_gather(landed, "dp", axis=0, tiled=True),
-        preferred_element_type=jnp.float32,
+    down_total = product_in_turn(
+        landed,
+        "dp",
+        0,
+        lambda part, at: jnp.einsum(
+            "rf,rd->fd",
+            lax.dynamic_slice_in_dim(hidden, at, part.shape[0], axis=0),
+            part,
+            preferred_element_type=jnp.float32,
+        ),
     )
     return (down_total.astype(jnp.bfloat16)[None], key_value_grad)
 

time: 633 us -> 578 us (0.913)
  waiting for transfers between devices: 435 us -> 326 us
  starting transfers between devices: 7.63 us -> 66.2 us
  blocking collectives: 114 us -> 101 us
  matrix products: 5.81 us -> 13.9 us
    all_gather x1 -> x0, waiting for transfers between devices: 71.5 us -> none  [per_device(): lax.all_gather(landed, 'dp', axis=0, tiled=True)]
    unnamed x7 -> x6, waiting for transfers between devices: 190 us -> 135 us
    ppermute x0 -> x15, starting transfers between devices: none -> 52.5 us  [the longest x7 37.2 us: product_in_turn(): from_right = lax.ppermute(from_right, axis, left)]
    all_to_all x1 -> x0, blocking collectives: 12.6 us -> none  [per_device(): lax.all_to_all(grad_slots, 'expert', split_axis=0, concat_axis=2, tiled=T...]
    ppermute x0 -> x15, waiting for transfers between devices: none -> 12.1 us  [the longest x8 12 us: product_in_turn(): from_left = lax.ppermute(from_left, axis, right)]
    dot_general x1 -> x16, matrix products: 1.43 us -> 8.49 us  [per_device(): jnp.einsum('rf,rd->fd', lax.dynamic_slice_in_dim(hidden, at, part.shape[0...]
  transfers between devices with their start and end apart: 6 -> 21, of which waited for: 6 -> 12; matrix products, arithmetic and copies ran while one was open for 1% -> 2% of each run, Pallas kernels for 0% -> 0%
where the time goes in v1:
time: 578 us; the launch traced here: 577 us
  waiting for transfers between devices  326 us (56%)
  blocking collectives  101 us (17%)
  starting transfers between devices  66.2 us (11%)
  other arithmetic  29.4 us (5%)
  local copies, waits for them, and re-layouts  24.1 us (4%)
  between operations  15.4 us (3%)
  matrix products  13.9 us (2%)
    unnamed x6, waiting for transfers between devices  135 us
    reduce_scatter x1, waiting for transfers between devices, per_device(): lax.psum_scatter(proj_term.astype(jnp.bfloat16), 'expert', scatter_dimens...  93.3 us
    all_gather x1, waiting for transfers between devices, per_device(): rows = lax.all_gather(arrived, 'dp', axis=0, tiled=True)  74.2 us
    psum x1, blocking collectives, per_device(): total_sq = lax.psum(jnp.sum(values * values, axis=1), 'expert')  63 us
    ppermute x7, starting transfers between devices, product_in_turn(): from_right = lax.ppermute(from_right, axis, left)  37.2 us
    unnamed x1, other arithmetic  23.4 us
    all_gather x1, blocking collectives, per_device(): cotangent = lax.all_gather(cotangent_cols, 'expert', axis=1, tiled=True)  23.1 us
    ppermute x8, starting transfers between devices, product_in_turn(): from_left = lax.ppermute(from_left, axis, right)  15.3 us
  transfers between devices with their start and end apart: 21, of which 12 were waited for; matrix products, arithmetic and copies ran while one was open for 2% of the time, Pallas kernels for 0%

profile of v1, /device:TPU:2, one launch (start us, length us, event | category | flops | bytes accessed | tf_op | source)
XLA Modules:
  0.0 576.6 jit_solution(6795519435441768480)
XLA Ops:
  7.2 0.9 copy.34
  9.1 0.9 fusion.14
  9.9 63.0 %psum.7 = f32[128]{0:T(128)S(1)} all-reduce(f32[128]{0:T(128)S(1)} %fusion.14), channel_id=1, replica_groups=mesh['dp'=16,'expert'=32] {'expert'}, use_global_device_ids=true, to_apply=%region_4.5 | all-reduce | flops 128 | bytes 1024 | tf_op jit(solution)/shard_map/psum | solution.py:59
  74.0 0.8 dynamic_slice.51
  74.8 0.8 fusion.16
  75.8 1.2 scatter_custom_fusion
  77.0 15.1 %all_to_all.45 = bf16[32,10,128]{2,1,0:T(8,128)(2,1)S(1)} all-to-all(bf16[32,10,128]{2,1,0:T(8,128)(2,1)S(1)} %reshape.83), channel_id=1, replica_groups=mesh['dp'=16,'expert'=32] {'expert'}, dimensions={0} | all-to-all | bytes 163840 | tf_op jit(solution)/shard_map/all_to_all | solution.py:64
  92.9 74.2 %all-gather.3.cloned.1.call-done = bf16[16,10,4096]{2,1,0:T(8,128)(2,1)} async-done(((bf16[1,10,4096]{2,1,0:T(8,128)(2,1)}), bf16[16,10,4096]{2,1,0:T(8,128)(2,1)}) %all-gather.3.cloned.1.call-update) | async-done | bytes 1310736 | tf_op jit(solution)/shard_map/all_gather | solution.py:65
  167.1 1.8 reshape.113
  170.6 1.6 convolution_convert_fusion
  172.4 1.3 dynamic-slice
  174.3 135.3 %all-reduce.3.cloned.1.call-done = bf16[160,4096]{1,0:T(8,128)(2,1)} async-done(((bf16[160,4096]{1,0:T(8,128)(2,1)}), bf16[160,4096]{1,0:T(8,128)(2,1)}) %all-reduce.3.cloned.1.call-update) | async-done | bytes 1310736
  309.6 1.0 dynamic-slice_bitcast_fusion
  310.5 2.8 copy.38
  313.9 23.4 %reduce.2 = bf16[4096,10]{1,0:T(8,128)(2,1)} reduce(bf16[4096,1,10]{2,1,0:T(2,128)(2,1)S(1)} %bitcast.90, bf16[]{:T(256)} %broadcast.89), dimensions={1}, to_apply=%bitcast.63.reduce_sub_computation | reduce | bytes 163842
  337.3 3.4 reshape.123
  340.7 7.4 %all-to-all-start.1 = ((bf16[32,2,640]{2,1,0:T(2,128)(2,1)}), bf16[32,2,640]{2,1,0:T(2,128)(2,1)S(1)}, u32[]{:S(2)}, u32[]{:S(2)}) async-start(bf16[32,2,640]{2,1,0:T(2,128)(2,1)} %reshape.123), calls=%async_computation.1 | async-start | bytes 163840 | tf_op jit(solution)/shard_map/all_to_all | solution.py:75
  348.2 6.3 %all-to-all-done.1 = bf16[32,2,640]{2,1,0:T(2,128)(2,1)S(1)} async-done(((bf16[32,2,640]{2,1,0:T(2,128)(2,1)}), bf16[32,2,640]{2,1,0:T(2,128)(2,1)S(1)}, u32[]{:S(2)}, u32[]{:S(2)}) %all-to-all-start.1) | async-done | bytes 81952 | tf_op jit(solution)/shard_map/all_to_all | solution.py:75
  354.4 2.2 reshape.124
  356.7 2.1 copy.39
  359.0 0.9 gather_fusion
  360.1 2.2 convolution_convert_fusion.2
  362.8 93.3 %reduce-scatter.5.cloned.1.call-done = bf16[128,64]{0,1:T(8,128)(2,1)} async-done(((bf16[128,2048]{0,1:T(8,128)(2,1)}), bf16[128,64]{0,1:T(8,128)(2,1)}) %reduce-scatter.5.cloned.1.call-update) | async-done | bytes 16400 | tf_op jit(solution)/shard_map/reduce_scatter | solution.py:80
  456.1 0.7 multiply_convert_fusion.2
  456.9 23.1 %all_gather.7 = bf16[128,2048]{0,1:T(8,128)(2,1)S(1)} all-gather(bf16[128,64]{0,1:T(8,128)(2,1)S(1)} %multiply_convert_fusion.2), channel_id=1, replica_groups=mesh['dp'=16,'expert'=32] {'expert'}, dimensions={1}, use_global_device_ids=true | all-gather | bytes 540672 | tf_op jit(solution)/shard_map/all_gather | solution.py:87
  480.4 1.3 scatter_custom_fusion.1
  482.4 6.1 %all-to-all-start.2 = ((bf16[32,10,128]{2,1,0:T(8,128)(2,1)}), bf16[32,10,128]{2,1,0:T(8,128)(2,1)S(1)}, u32[]{:S(2)}, u32[]{:S(2)}) async-start(bf16[32,10,128]{2,1,0:T(8,128)(2,1)} %reshape.86), calls=%async_computation.3 | async-start | bytes 262144 | tf_op jit(solution)/shard_map/all_to_all | solution.py:99
  488.9 1.0 copy.44
  489.9 5.2 all-to-all-done.2
  495.2 6.0 %collective-permute-start = (bf16[10,4096]{1,0:T(8,128)(2,1)S(1)}, bf16[10,4096]{1,0:T(8,128)(2,1)S(1)}, u32[]{:S(2)}, u32[]{:S(2)}) collective-permute-start(bf16[10,4096]{1,0:T(8,128)(2,1)S(1)} %bitcast.93), channel_id=1, source_target_pairs={{0,480},{32,0},{64,32},{96,64},{128,96},{160,128},{192,160},{224,1... | collective-permute-start | bytes 245768 | tf_op jit(solution)/shard_map/ppermute | solution.py:19
  501.2 1.9 collective-permute-start.1
  503.6 6.0 %collective-permute-done.1 = bf16[10,4096]{1,0:T(8,128)(2,1)S(1)} collective-permute-done((bf16[10,4096]{1,0:T(8,128)(2,1)S(1)}, bf16[10,4096]{1,0:T(8,128)(2,1)S(1)}, u32[]{:S(2)}, u32[]{:S(2)}) %collective-permute-start.1) | collective-permute-done | bytes 81952 | tf_op jit(solution)/shard_map/ppermute | solution.py:17
  509.6 1.9 collective-permute-start.3
  511.5 5.1 collective-permute-start.2
  517.9 1.9 collective-permute-start.5
  520.3 5.1 collective-permute-start.4
  526.2 1.9 collective-permute-start.7
  528.6 5.1 collective-permute-start.6
  534.3 1.9 collective-permute-start.9
  536.7 5.4 collective-permute-start.8
  542.6 1.9 collective-permute-start.11
  545.0 5.3 collective-permute-start.10
  550.8 1.9 collective-permute-start.13
  553.2 5.2 collective-permute-start.12
  559.0 1.9 collective-permute-start.14
  561.9 5.2 collective-permute-done.14
  567.1 1.4 fusion.7
  568.5 0.9 copy.45
  (90 shorter events, 16.1 us)
Async XLA Ops:
  7.2 163.4 %copy-start = (bf16[1,128,4096]{2,1,0:T(8,128)(2,1)S(1)}, bf16[1,128,4096]{2,1,0:T(8,128)(2,1)}, u32[]{:S(2)}) copy-start(bf16[1,128,4096]{2,1,0:T(8,128)(2,1)} %param.16) | copy-start | bytes 3145732
  7.2 159.9 %all-gather.3.cloned.1.call-start = ((), (), s32[]{:S(2)}) async-start(), calls=%async_computation.6 | async-start | bytes 2228224 | tf_op jit(solution)/shard_map/all_gather | solution.py:65
  77.0 91.8 %copy-start.2 = (bf16[1,4096,128]{2,1,0:T(8,128)(2,1)S(1)}, bf16[1,4096,128]{2,1,0:T(8,128)(2,1)}, u32[]{:S(2)}) copy-start(bf16[1,4096,128]{2,1,0:T(8,128)(2,1)} %param.14) | copy-start | bytes 3145732
  92.9 216.7 %all-reduce.3.cloned.1.call-start = ((), (), s32[]{:S(2)}) async-start(), calls=%async_computation.8 | async-start | bytes 2621440
  168.9 1.2 copy-start.3
  170.6 1.6 copy-start.6
  340.7 13.8 %all-to-all-start.1 = ((bf16[32,2,640]{2,1,0:T(2,128)(2,1)}), bf16[32,2,640]{2,1,0:T(2,128)(2,1)S(1)}, u32[]{:S(2)}, u32[]{:S(2)}) async-start(bf16[32,2,640]{2,1,0:T(2,128)(2,1)} %reshape.123), calls=%async_computation.1 | async-start | bytes 163840 | tf_op jit(solution)/shard_map/all_to_all | solution.py:75
  348.1 108.0 %reduce-scatter.5.cloned.1.call-start = ((), (), s32[]{:S(2)}) async-start(), calls=%async_computation.5 | async-start | bytes 540672 | tf_op jit(solution)/shard_map/reduce_scatter | solution.py:80
  356.7 3.4 copy-start.4
  358.8 3.9 copy-start.7
  358.9 97.3 %copy-start.5 = (bf16[128,64]{0,1:T(8,128)(2,1)S(1)}, bf16[128,64]{0,1:T(8,128)(2,1)}, u32[]{:S(2)}) copy-start(bf16[128,64]{0,1:T(8,128)(2,1)} %param.18) | copy-start | bytes 49156
  358.9 121.1 %copy-start.1 = (bf16[128,2048]{1,0:T(8,128)(2,1)S(1)}, bf16[128,2048]{1,0:T(8,128)(2,1)}, u32[]{:S(2)}) copy-start(bf16[128,2048]{1,0:T(8,128)(2,1)} %param.17) | copy-start | bytes 1572868
  482.4 12.8 %all-to-all-start.2 = ((bf16[32,10,128]{2,1,0:T(8,128)(2,1)}), bf16[32,10,128]{2,1,0:T(8,128)(2,1)S(1)}, u32[]{:S(2)}, u32[]{:S(2)}) async-start(bf16[32,10,128]{2,1,0:T(8,128)(2,1)} %reshape.86), calls=%async_computation.3 | async-start | bytes 262144 | tf_op jit(solution)/shard_map/all_to_all | solution.py:99
  488.5 80.0 %reduce-scatter.7.cloned.1.call-start = ((), (), s32[]{:S(2)}) async-start(), calls=%async_computation.7 | async-start | bytes 557056
  495.2 16.3 %collective-permute-start = (bf16[10,4096]{1,0:T(8,128)(2,1)S(1)}, bf16[10,4096]{1,0:T(8,128)(2,1)S(1)}, u32[]{:S(2)}, u32[]{:S(2)}) collective-permute-start(bf16[10,4096]{1,0:T(8,128)(2,1)S(1)} %bitcast.93), channel_id=1, source_target_pairs={{0,480},{32,0},{64,32},{96,64},{128,96},{160,128},{192,160},{224,1... | collective-permute-start | bytes 245768 | tf_op jit(solution)/shard_map/ppermute | solution.py:19
  501.2 8.4 %collective-permute-start.1 = (bf16[10,4096]{1,0:T(8,128)(2,1)S(1)}, bf16[10,4096]{1,0:T(8,128)(2,1)S(1)}, u32[]{:S(2)}, u32[]{:S(2)}) collective-permute-start(bf16[10,4096]{1,0:T(8,128)(2,1)S(1)} %bitcast.94), channel_id=1, source_target_pairs={{0,32},{32,64},{64,96},{96,128},{128,160},{160,192},{192,224},{224... | collective-permute-start | bytes 245768 | tf_op jit(solution)/shard_map/ppermute | solution.py:17
  509.6 8.3 %collective-permute-start.3 = (bf16[10,4096]{1,0:T(8,128)(2,1)S(1)}, bf16[10,4096]{1,0:T(8,128)(2,1)S(1)}, u32[]{:S(2)}, u32[]{:S(2)}) collective-permute-start(bf16[10,4096]{1,0:T(8,128)(2,1)S(1)} %collective-permute-done.1), channel_id=1, source_target_pairs={{0,32},{32,64},{64,96},{96,128},{128,160},{160,192},{192,224},{224... | collective-permute-start | bytes 245768 | tf_op jit(solution)/shard_map/ppermute | solution.py:17
  511.5 8.8 %collective-permute-start.2 = (bf16[10,4096]{1,0:T(8,128)(2,1)S(1)}, bf16[10,4096]{1,0:T(8,128)(2,1)S(1)}, u32[]{:S(2)}, u32[]{:S(2)}) collective-permute-start(bf16[10,4096]{1,0:T(8,128)(2,1)S(1)} %collective-permute-done), channel_id=1, source_target_pairs={{0,480},{32,0},{64,32},{96,64},{128,96},{160,128},{192,160},{224,1... | collective-permute-start | bytes 245768 | tf_op jit(solution)/shard_map/ppermute | solution.py:19
  517.9 8.2 %collective-permute-start.5 = (bf16[10,4096]{1,0:T(8,128)(2,1)S(1)}, bf16[10,4096]{1,0:T(8,128)(2,1)S(1)}, u32[]{:S(2)}, u32[]{:S(2)}) collective-permute-start(bf16[10,4096]{1,0:T(8,128)(2,1)S(1)} %collective-permute-done.3), channel_id=1, source_target_pairs={{0,32},{32,64},{64,96},{96,128},{128,160},{160,192},{192,224},{224... | collective-permute-start | bytes 245768 | tf_op jit(solution)/shard_map/ppermute | solution.py:17
  520.3 8.2 %collective-permute-start.4 = (bf16[10,4096]{1,0:T(8,128)(2,1)S(1)}, bf16[10,4096]{1,0:T(8,128)(2,1)S(1)}, u32[]{:S(2)}, u32[]{:S(2)}) collective-permute-start(bf16[10,4096]{1,0:T(8,128)(2,1)S(1)} %collective-permute-done.2), channel_id=1, source_target_pairs={{0,480},{32,0},{64,32},{96,64},{128,96},{160,128},{192,160},{224,1... | collective-permute-start | bytes 245768 | tf_op jit(solution)/shard_map/ppermute | solution.py:19
  526.2 8.1 %collective-permute-start.7 = (bf16[10,4096]{1,0:T(8,128)(2,1)S(1)}, bf16[10,4096]{1,0:T(8,128)(2,1)S(1)}, u32[]{:S(2)}, u32[]{:S(2)}) collective-permute-start(bf16[10,4096]{1,0:T(8,128)(2,1)S(1)} %collective-permute-done.5), channel_id=1, source_target_pairs={{0,32},{32,64},{64,96},{96,128},{128,160},{160,192},{192,224},{224... | collective-permute-start | bytes 245768 | tf_op jit(solution)/shard_map/ppermute | solution.py:17
  528.6 8.1 %collective-permute-start.6 = (bf16[10,4096]{1,0:T(8,128)(2,1)S(1)}, bf16[10,4096]{1,0:T(8,128)(2,1)S(1)}, u32[]{:S(2)}, u32[]{:S(2)}) collective-permute-start(bf16[10,4096]{1,0:T(8,128)(2,1)S(1)} %collective-permute-done.4), channel_id=1, source_target_pairs={{0,480},{32,0},{64,32},{96,64},{128,96},{160,128},{192,160},{224,1... | collective-permute-start | bytes 245768 | tf_op jit(solution)/shard_map/ppermute | solution.py:19
  534.3 8.3 %collective-permute-start.9 = (bf16[10,4096]{1,0:T(8,128)(2,1)S(1)}, bf16[10,4096]{1,0:T(8,128)(2,1)S(1)}, u32[]{:S(2)}, u32[]{:S(2)}) collective-permute-start(bf16[10,4096]{1,0:T(8,128)(2,1)S(1)} %collective-permute-done.7), channel_id=1, source_target_pairs={{0,32},{32,64},{64,96},{96,128},{128,160},{160,192},{192,224},{224... | collective-permute-start | bytes 245768 | tf_op jit(solution)/shard_map/ppermute | solution.py:17
  536.7 8.3 %collective-permute-start.8 = (bf16[10,4096]{1,0:T(8,128)(2,1)S(1)}, bf16[10,4096]{1,0:T(8,128)(2,1)S(1)}, u32[]{:S(2)}, u32[]{:S(2)}) collective-permute-start(bf16[10,4096]{1,0:T(8,128)(2,1)S(1)} %collective-permute-done.6), channel_id=1, source_target_pairs={{0,480},{32,0},{64,32},{96,64},{128,96},{160,128},{192,160},{224,1... | collective-permute-start | bytes 245768 | tf_op jit(solution)/shard_map/ppermute | solution.py:19
  542.6 8.2 %collective-permute-start.11 = (bf16[10,4096]{1,0:T(8,128)(2,1)S(1)}, bf16[10,4096]{1,0:T(8,128)(2,1)S(1)}, u32[]{:S(2)}, u32[]{:S(2)}) collective-permute-start(bf16[10,4096]{1,0:T(8,128)(2,1)S(1)} %collective-permute-done.9), channel_id=1, source_target_pairs={{0,32},{32,64},{64,96},{96,128},{128,160},{160,192},{192,224},{224... | collective-permute-start | bytes 245768 | tf_op jit(solution)/shard_map/ppermute | solution.py:17
  545.0 8.2 %collective-permute-start.10 = (bf16[10,4096]{1,0:T(8,128)(2,1)S(1)}, bf16[10,4096]{1,0:T(8,128)(2,1)S(1)}, u32[]{:S(2)}, u32[]{:S(2)}) collective-permute-start(bf16[10,4096]{1,0:T(8,128)(2,1)S(1)} %collective-permute-done.8), channel_id=1, source_target_pairs={{0,480},{32,0},{64,32},{96,64},{128,96},{160,128},{192,160},{224,1... | collective-permute-start | bytes 245768 | tf_op jit(solution)/shard_map/ppermute | solution.py:19
  550.8 8.2 %collective-permute-start.13 = (bf16[10,4096]{1,0:T(8,128)(2,1)S(1)}, bf16[10,4096]{1,0:T(8,128)(2,1)S(1)}, u32[]{:S(2)}, u32[]{:S(2)}) collective-permute-start(bf16[10,4096]{1,0:T(8,128)(2,1)S(1)} %collective-permute-done.11), channel_id=1, source_target_pairs={{0,32},{32,64},{64,96},{96,128},{128,160},{160,192},{192,224},{224... | collective-permute-start | bytes 245768 | tf_op jit(solution)/shard_map/ppermute | solution.py:17
  553.2 8.2 %collective-permute-start.12 = (bf16[10,4096]{1,0:T(8,128)(2,1)S(1)}, bf16[10,4096]{1,0:T(8,128)(2,1)S(1)}, u32[]{:S(2)}, u32[]{:S(2)}) collective-permute-start(bf16[10,4096]{1,0:T(8,128)(2,1)S(1)} %collective-permute-done.10), channel_id=1, source_target_pairs={{0,480},{32,0},{64,32},{96,64},{128,96},{160,128},{192,160},{224,1... | collective-permute-start | bytes 245768 | tf_op jit(solution)/shard_map/ppermute | solution.py:19
  559.0 8.1 %collective-permute-start.14 = (bf16[10,4096]{1,0:T(8,128)(2,1)S(1)}, bf16[10,4096]{1,0:T(8,128)(2,1)S(1)}, u32[]{:S(2)}, u32[]{:S(2)}) collective-permute-start(bf16[10,4096]{1,0:T(8,128)(2,1)S(1)} %collective-permute-done.13), channel_id=1, source_target_pairs={{0,32},{32,64},{64,96},{96,128},{128,160},{160,192},{192,224},{224... | collective-permute-start | bytes 245768 | tf_op jit(solution)/shard_map/ppermute | solution.py:17
Sparse Core Ops, SparseCore 0:
  93.0 74.0 all-gather.2
  172.4 137.1 all-reduce.2
  362.5 93.6 reduce-scatter.4
  491.8 70.9 reduce-scatter.6
